TPU v7x, 128 devices: a whole 4x4x4 slice. The times are simulated.
128 devices in a mesh: slot: 32 (over y, z, core), hid: 4 (over x).
Axes of the slice: x: 4, y: 4, z: 4, core: 2. Of those that a mesh axis runs over, the one named last changes fastest.
Arguments:
- master: float32 [16, 3, 4, 393216], P(None, None, 'hid', 'slot'), may hold values from -0.125 to 0.125
- first_moment: float32 [16, 3, 4, 393216], P(None, None, 'hid', 'slot'), may hold values from -0.3 to 0.3
- second_moment: float32 [16, 3, 4, 393216], P(None, None, 'hid', 'slot'), may hold values from 0.0001 to 0.01
- slot_weights: bfloat16 [32, 3, 768, 2048], P('slot', None, 'hid'), may hold values from -0.125 to 0.125
- back_rows: bfloat16 [32, 1024, 2048], P('slot'), may hold values from -6 to 6
- readout: bfloat16 [32, 1024, 2048], P('slot'), may hold values from -0.25 to 0.25
- ref_logratio: float32 [32, 1024], P('slot'), may hold values from -9 to 0
- labels: int32 [32, 1024], P('slot'), may hold values 0 or 1
- place_cur: int32 [32], replicated, may hold values from 0 to 15, as said below
- place_next: int32 [32], replicated, may hold values from 0 to 15, as said below
- fwd_rows: bfloat16 [8192, 2048], P('slot', 'hid'), may hold values from -6 to 6
- routes: int32 [8192, 1], P('slot'), may hold values from 0 to 31; in each aligned block of 256 rows (0 to 255, 256 to 511, ...) at most 16 rows name the same one
Outputs:
- out_rows: bfloat16 [8192, 2048], P('slot', 'hid')
- new_master: float32 [16, 3, 4, 393216], P(None, None, 'hid', 'slot')
- new_first: float32 [16, 3, 4, 393216], P(None, None, 'hid', 'slot')
- new_second: float32 [16, 3, 4, 393216], P(None, None, 'hid', 'slot')
Inputs may be any that keep to these rules, and one draw needn't show every extreme that they name: `place_cur`: every expert 0 to 15 is held by at least one slot. `place_next`: every expert 0 to 15 is held by at least one slot. `routes`: the rows of one slot name any one slot at most 16 times, a bound that some block reaches.
All inputs are finite; a program needn't handle non-finite values. No bound on the sum of `labels` on one device may be relied on, other than what follows from the above.
Results may differ from a plain program's by a relative error of at most 0.008.
Values may be sent and summed in bfloat16 or wider, within the bound.
No kernel may reach another device: no remote copies, remote signals or barrier semaphores. Data moves between devices by JAX's collectives and lax.ppermute only.
A program may use at most 128 MiB of HBM per device.

v0:
```python
import jax
import jax.numpy as jnp
from jax import lax
from jax.sharding import PartitionSpec as P

beta_kto = 1.0
desired_weight = 1.0
undesired_weight = 1.33
learn_rate = 0.004
decay_first = 0.9
decay_second = 0.999
correct_first = 0.9999734386011124
correct_second = 0.09520785288629043
adam_eps = 1e-08
weight_decay = 0.1


def expert_pass(inputs, weights):
    across = (((1,), (1,)), ((), ()))
    gate_vals = lax.dot_general(inputs, weights[0], across, preferred_element_type=jnp.float32)
    up_vals = lax.dot_general(inputs, weights[1], across, preferred_element_type=jnp.float32)
    hidden = (gate_vals * jax.nn.sigmoid(gate_vals) * up_vals).astype(jnp.bfloat16)
    produced = jnp.dot(hidden, weights[2], preferred_element_type=jnp.float32)
    return (gate_vals, up_vals, hidden, produced)


def kto_slope(scores, labels, center):
    sigma_v = jax.nn.sigmoid(beta_kto * (scores - center))
    signed = jnp.where(labels == 1, -desired_weight, undesired_weight)
    return beta_kto * sigma_v * (1.0 - sigma_v) * signed


def expert_backward(inputs, direction, weights, slope, gate_vals, up_vals, hidden):
    d_expert = (slope[:, None] * direction.astype(jnp.float32)).astype(jnp.bfloat16)
    d_hidden = lax.dot_general(
        d_expert, weights[2], (((1,), (1,)), ((), ())), preferred_element_type=jnp.float32
    )
    sigma_g = jax.nn.sigmoid(gate_vals)
    d_gate = (d_hidden * up_vals * sigma_g * (1.0 + gate_vals * (1.0 - sigma_g))).astype(
        jnp.bfloat16
    )
    d_up = (d_hidden * gate_vals * sigma_g).astype(jnp.bfloat16)
    contract = (((0,), (0,)), ((), ()))
    grad_gate = lax.dot_general(d_gate, inputs, contract, preferred_element_type=jnp.float32)
    grad_up = lax.dot_general(d_up, inputs, contract, preferred_element_type=jnp.float32)
    grad_down = lax.dot_general(hidden, d_expert, contract, preferred_element_type=jnp.float32)
    return jnp.stack([grad_gate, grad_up, grad_down])


def adamw_update(master, first_moment, second_moment, summed):
    new_first = decay_first * first_moment + (1.0 - decay_first) * summed
    new_second = decay_second * second_moment + (1.0 - decay_second) * summed * summed
    update = new_first / correct_first / (jnp.sqrt(new_second / correct_second) + adam_eps)
    new_master = master - learn_rate * (update + weight_decay * master)
    return (new_master, new_first, new_second)


def shards(
    master,
    first_moment,
    second_moment,
    slot_weights,
    back_rows,
    readout,
    ref_logratio,
    labels,
    place_cur,
    place_next,
    fwd_rows,
    routes,
):
    slot_count = lax.axis_size("slot")
    experts_here = master.shape[0]
    weights = slot_weights[0]
    width = weights.shape[2]
    owned_units = master.shape[3] // width
    inputs = back_rows[0]
    direction = readout[0]
    gate_vals, up_vals, hidden, partial_value = expert_pass(inputs, weights)
    row_part = jnp.sum(partial_value * direction.astype(jnp.float32), axis=1)
    policy = lax.psum(row_part, "hid")
    scores = policy - ref_logratio[0]
    row_total = slot_count * inputs.shape[0]
    center = lax.psum(jnp.sum(scores), "slot") / row_total
    slope = kto_slope(scores, labels[0], center)
    grads = expert_backward(inputs, direction, weights, slope, gate_vals, up_vals, hidden)
    arrived = lax.all_to_all(
        grads[None].astype(jnp.bfloat16), "slot", split_axis=2, concat_axis=0, tiled=True
    ).astype(jnp.float32)
    arrived = arrived.reshape(slot_count, 3, 1, owned_units * width)
    owner_map = (place_cur[None, :] == jnp.arange(experts_here, dtype=jnp.int32)[:, None]).astype(
        jnp.float32
    )
    summed = jnp.einsum("es,sabc->eabc", owner_map, arrived, precision=lax.Precision.HIGHEST)
    new_master, new_first, new_second = adamw_update(master, first_moment, second_moment, summed)
    refreshed = new_master.astype(jnp.bfloat16)
    pick_map = (place_next[:, None] == jnp.arange(experts_here, dtype=jnp.int32)[None, :]).astype(
        jnp.bfloat16
    )
    picked = jnp.einsum(
        "se,eabc->sabc", pick_map, refreshed, preferred_element_type=jnp.float32
    ).astype(jnp.bfloat16)
    picked = picked.reshape(slot_count, 3, owned_units, width)
    resident = lax.all_to_all(picked, "slot", split_axis=0, concat_axis=2, tiled=True)[0]
    capacity = 2 * fwd_rows.shape[0] // slot_count
    quarter = fwd_rows.shape[1]
    target = routes[:, 0]
    target_map = (target[:, None] == jnp.arange(slot_count, dtype=jnp.int32)[None, :]).astype(
        jnp.int32
    )
    earlier = jnp.cumsum(target_map, axis=0) - target_map
    position = jnp.sum(earlier * target_map, axis=1)
    slot_place = target * capacity + position
    place_map = (
        slot_place[None, :] == jnp.arange(slot_count * capacity, dtype=jnp.int32)[:, None]
    ).astype(jnp.bfloat16)
    widened = lax.all_gather(fwd_rows, "hid", axis=1, tiled=True)
    buffer_rows = jnp.dot(place_map, widened, preferred_element_type=jnp.float32).astype(
        jnp.bfloat16
    )
    buffer_rows = buffer_rows.reshape(slot_count, capacity, widened.shape[1])
    arrived_rows = lax.all_to_all(
        buffer_rows, "slot", split_axis=0, concat_axis=0, tiled=True
    ).reshape(slot_count * capacity, widened.shape[1])
    fwd_partial = expert_pass(arrived_rows, resident)[3]
    totals = lax.psum(fwd_partial, "hid")
    shares = lax.dynamic_slice_in_dim(totals, lax.axis_index("hid") * quarter, quarter, 1)
    outgoing = shares.astype(jnp.bfloat16).reshape(slot_count, capacity, quarter)
    returned = lax.all_to_all(outgoing, "slot", split_axis=0, concat_axis=0, tiled=True).reshape(
        slot_count * capacity, quarter
    )
    out_rows = lax.dot_general(
        place_map, returned, (((0,), (0,)), ((), ())), preferred_element_type=jnp.float32
    ).astype(jnp.bfloat16)
    return (out_rows, new_master, new_first, new_second)


def solution(mesh):
    return jax.shard_map(
        shards,
        mesh=mesh,
        in_specs=(
            P(None, None, "hid", "slot"),
            P(None, None, "hid", "slot"),
            P(None, None, "hid", "slot"),
            P("slot", None, "hid", None),
            P("slot", None, None),
            P("slot", None, None),
            P("slot", None),
            P("slot", None),
            P(),
            P(),
            P("slot", "hid"),
            P("slot", None),
        ),
        out_specs=(
            P("slot", "hid"),
            P(None, None, "hid", "slot"),
            P(None, None, "hid", "slot"),
            P(None, None, "hid", "slot"),
        ),
        check_vma=False,
    )
```

profile of v0, /device:TPU:1, one launch (start us, length us, event | category | flops | bytes accessed | tf_op | source)
XLA Modules:
  0.0 364.6 jit_solution(15891182138285590733)
XLA Ops:
  7.2 0.0 copy-start.11
  7.2 0.0 copy-start.13
  7.2 4.1 %fusion.16 = f32[1024,192]{0,1:T(8,128)S(1)} fusion(bf16[1,1024,2048]{2,1,0:T(8,128)(2,1)} %param.16, bf16[1,3,192,2048]{3,2,1,0:T(8,128)(2,1)} %param.15), kind=kOutput, calls=%fused_computation.17 | convolution fusion | flops 805306368 | bytes 5767168 | tf_op jit(solution)/shard_map/dot_general | solution.py:20
  11.3 0.0 copy-done.11
  11.3 0.3 copy-done.13
  11.6 2.5 multiply_convert_fusion.2
  14.1 0.0 copy-done.9
  14.1 1.4 fusion.2
  15.5 9.3 %psum.21 = f32[1024]{0:T(1024)S(1)} all-reduce(f32[1024]{0:T(1024)S(1)} %fusion.2), channel_id=1, replica_groups=mesh['slot'=32,'hid'=4] {'hid'}, use_global_device_ids=true, to_apply=%region_4.5 | all-reduce | flops 1024 | bytes 8192 | tf_op jit(solution)/shard_map/psum | solution.py:81
  24.8 0.0 copy-done.6
  24.8 0.6 fusion.78
  25.4 66.9 %psum.22 = f32[]{:T(128)} all-reduce(f32[]{:T(128)} %get-tuple-element.19), channel_id=1, replica_groups=mesh['slot'=32,'hid'=4] {'slot'}, use_global_device_ids=true, to_apply=%region_6.7 | all-reduce | flops 1 | bytes 8 | tf_op jit(solution)/shard_map/psum | solution.py:84
  92.3 0.0 copy-done.7
  93.0 0.0 copy-start.10
  93.0 4.0 %fusion.6 = f32[1024,192]{0,1:T(8,128)S(1)} fusion(bf16[1,1024,2048]{2,1,0:T(8,128)(2,1)} %param.17, f32[1024]{0:T(1024)S(1)} %fusion.71, bf16[1,3,192,2048]{3,2,1,0:T(8,128)(2,1)S(1)} %copy-done.13), kind=kOutput, calls=%fused_computation.9 | convolution fusion | flops 811597824 | bytes 5771264 | tf_op jit(solution)/shard_map/dot_general | solution.py:35
  96.9 0.0 copy-done.10
  96.9 0.0 copy-start.12
  96.9 1.2 fusion.35
  98.1 1.0 copy-done.12
  99.1 1.1 fusion.29
  100.2 0.1 copy-done.15
  100.3 1.2 fusion.32
  101.5 0.3 pad_maximum_fusion
  101.7 2.0 copy.33
  103.8 45.2 %all_to_all.40 = bf16[1,3,192,2048]{3,1,0,2:T(4,128)(2,1)S(1)} all-to-all(bf16[1,3,192,2048]{3,1,0,2:T(4,128)(2,1)S(1)} %copy.33), channel_id=1, replica_groups=mesh['slot'=32,'hid'=4] {'slot'}, dimensions={2} | all-to-all | bytes 4718592 | tf_op jit(solution)/shard_map/all_to_all | solution.py:87
  148.9 1.7 copy.55
  150.6 0.0 copy-start.14
  150.7 4.5 %reshape.144 = bf16[32,3,12288]{2,0,1:T(8,128)(2,1)} reshape(bf16[32,1,3,6,2048]{4,3,0,2,1:T(8,128)(2,1)S(1)} %bitcast.131) | data formatting | bytes 4718592 | tf_op jit(solution)/shard_map/reshape.20
  155.2 0.0 copy-done.14
  155.2 11.4 %multiply_subtract_fusion = (f32[16,3,1,12288]{3,0,1,2:T(8,128)S(1)}, f32[16,3,1,12288]{3,0,1,2:T(8,128)}, f32[16,3,1,12288]{3,0,1,2:T(8,128)}) fusion(f32[16,3,1,12288]{3,2,1,0:T(1,128)} %param.12, f32[16,3,1,12288]{3,2,1,0:T(1,128)} %param.13, f32[16,3,1,12288]{3,2,1,0:T(1,128)} %param.14, bf16[32,3,12288]{2,0,1:T(8,128)(2,1)} %reshape.144, ...), kind=kOutput, calls=%fused_computation.36 | convolution fusion | flops 46596608 | bytes 16515200 | tf_op jit(solution)/shard_map/es,sabc->eabc/dot_general | solution.py:94
  166.5 1.4 copy-done
  167.9 0.0 copy-done.8
  167.9 2.2 convolution_convert_fusion
  170.2 5.0 %reshape.146 = bf16[32,3,6,2048]{3,2,0,1:T(8,128)(2,1)S(1)} reshape(bf16[32,3,12288]{2,0,1:T(8,128)(2,1)} %convolution_convert_fusion) | data formatting | bytes 4718592 | tf_op jit(solution)/shard_map/reshape | solution.py:103
  175.1 1.9 copy.38
  177.0 4.0 %all-to-all-start.2 = ((bf16[32,3,6,2048]{3,2,1,0:T(8,128)(2,1)}), bf16[32,3,6,2048]{3,2,1,0:T(8,128)(2,1)S(1)}, u32[]{:S(2)}, u32[]{:S(2)}) async-start(bf16[32,3,6,2048]{3,2,1,0:T(8,128)(2,1)} %copy.38), calls=%async_computation.2 | async-start | bytes 6291456 | tf_op jit(solution)/shard_map/all_to_all | solution.py:104
  181.1 0.0 all-gather.2.cloned.1.call-start
  181.1 0.7 all-gather.2.cloned.1.call-update
  181.8 0.0 copy-done.5
  181.8 0.6 reduce-window.6
  182.4 0.2 slice_reduce_fusion
  182.6 0.1 fusion.64
  182.8 21.8 %all-gather.2.cloned.1.call-done = bf16[256,2048]{1,0:T(8,128)(2,1)} async-done(((bf16[256,512]{1,0:T(8,128)(2,1)}), bf16[256,2048]{1,0:T(8,128)(2,1)}) %all-gather.2.cloned.1.call-update) | async-done | bytes 1048592 | tf_op jit(solution)/shard_map/all_gather | solution.py:117
  204.6 3.3 convolution_convert_fusion.1
  207.9 13.0 %all-to-all-done.2 = bf16[32,3,6,2048]{3,2,1,0:T(8,128)(2,1)S(1)} async-done(((bf16[32,3,6,2048]{3,2,1,0:T(8,128)(2,1)}), bf16[32,3,6,2048]{3,2,1,0:T(8,128)(2,1)S(1)}, u32[]{:S(2)}, u32[]{:S(2)}) %all-to-all-start.2) | async-done | bytes 2359328 | tf_op jit(solution)/shard_map/all_to_all | solution.py:104
  220.8 5.3 %all-to-all-start = ((bf16[32,16,2048]{2,1,0:T(8,128)(2,1)}), bf16[32,16,2048]{2,1,0:T(8,128)(2,1)}, u32[]{:S(2)}, u32[]{:S(2)}) async-start(bf16[32,16,2048]{2,1,0:T(8,128)(2,1)} %bitcast.132), calls=%async_computation | async-start | bytes 4194304 | tf_op jit(solution)/shard_map/all_to_all | solution.py:122
  226.1 1.8 fusion.79
  227.9 1.5 squeeze.38
  229.4 1.4 squeeze.39
  230.8 0.3 squeeze.40
  231.0 23.5 %all-to-all-done = bf16[32,16,2048]{2,1,0:T(8,128)(2,1)} async-done(((bf16[32,16,2048]{2,1,0:T(8,128)(2,1)}), bf16[32,16,2048]{2,1,0:T(8,128)(2,1)}, u32[]{:S(2)}, u32[]{:S(2)}) %all-to-all-start) | async-done | bytes 2097184 | tf_op jit(solution)/shard_map/all_to_all | solution.py:122
  254.6 2.4 fusion.80
  257.0 5.1 %fusion.43 = f32[512,2048]{1,0:T(8,128)} fusion(bf16[192,2048]{1,0:T(8,128)(2,1)S(1)} %squeeze.40, bf16[512,2048]{1,0:T(8,128)(2,1)} %bitcast.4, bf16[192,2048]{1,0:T(8,128)(2,1)S(1)} %squeeze.39, f32[512,192]{0,1:T(8,128)S(1)} %fusion.80), kind=kOutput, calls=%fused_computation.42 | convolution fusion | flops 805896192 | bytes 8257536 | tf_op jit(solution)/shard_map/dot_general | solution.py:23
  262.1 75.4 %all-reduce.1 = bf16[512,2048]{1,0:T(8,128)(2,1)} all-reduce(f32[512,2048]{1,0:T(8,128)} %fusion.43), channel_id=1, replica_groups=mesh['slot'=32,'hid'=4] {'hid'}, use_global_device_ids=true, to_apply=%region_7.8 | all-reduce | flops 1048576 | bytes 6291456 | tf_op jit(solution)/shard_map/psum | solution.py:126
  337.6 1.9 dynamic-slice_convert_fusion
  339.4 5.5 %all-to-all-start.3 = ((bf16[32,16,512]{2,1,0:T(8,128)(2,1)}), bf16[32,16,512]{2,1,0:T(8,128)(2,1)S(1)}, u32[]{:S(2)}, u32[]{:S(2)}) async-start(bf16[32,16,512]{2,1,0:T(8,128)(2,1)} %bitcast.26), calls=%async_computation.3 | async-start | bytes 1048576 | tf_op jit(solution)/shard_map/all_to_all | solution.py:129
  345.0 0.0 copy-start.4
  345.0 3.8 %copy.39 = f32[16,3,1,12288]{3,2,1,0:T(1,128)} copy(f32[16,3,1,12288]{3,0,1,2:T(8,128)S(1)} %copy-done.1) | data formatting | bytes 4718592
  348.8 0.0 copy-done.4
  348.8 3.8 %copy.40 = f32[16,3,1,12288]{3,2,1,0:T(1,128)} copy(f32[16,3,1,12288]{3,0,1,2:T(8,128)S(1)} %copy-done.4) | data formatting | bytes 4718592
  352.7 0.0 copy-done.3
  352.7 3.8 %copy.41 = f32[16,3,1,12288]{3,2,1,0:T(1,128)} copy(f32[16,3,1,12288]{3,0,1,2:T(8,128)S(1)} %copy-done.3) | data formatting | bytes 4718592
  356.5 0.2 all-to-all-done.3
  356.7 1.1 convolution_convert_fusion.2
  (18 shorter events, 0.1 us)
Async XLA Ops:
  7.2 4.1 %copy-start.11 = (bf16[1,1024,2048]{2,1,0:T(8,128)(2,1)S(1)}, bf16[1,1024,2048]{2,1,0:T(8,128)(2,1)}, u32[]{:S(2)}) copy-start(bf16[1,1024,2048]{2,1,0:T(8,128)(2,1)} %param.16) | copy-start | bytes 12582916
  7.2 4.4 %copy-start.13 = (bf16[1,3,192,2048]{3,2,1,0:T(8,128)(2,1)S(1)}, bf16[1,3,192,2048]{3,2,1,0:T(8,128)(2,1)}, u32[]{:S(2)}) copy-start(bf16[1,3,192,2048]{3,2,1,0:T(8,128)(2,1)} %param.15) | copy-start | bytes 7077892
  11.6 2.5 copy-start.9
  14.1 10.7 %copy-start.6 = (f32[1,1024]{1,0:T(1,128)S(1)}, f32[1,1024]{1,0:T(1,128)}, u32[]{:S(2)}) copy-start(f32[1,1024]{1,0:T(1,128)} %param.18) | copy-start | bytes 12292
  14.1 78.2 %copy-start.7 = (s32[1,1024]{1,0:T(1,128)S(1)}, s32[1,1024]{1,0:T(1,128)}, u32[]{:S(2)}) copy-start(s32[1,1024]{1,0:T(1,128)} %param.19) | copy-start | bytes 12292
  93.0 4.0 %copy-start.10 = (bf16[1,1024,2048]{2,1,0:T(8,128)(2,1)S(1)}, bf16[1,1024,2048]{2,1,0:T(8,128)(2,1)}, u32[]{:S(2)}) copy-start(bf16[1,1024,2048]{2,1,0:T(8,128)(2,1)} %param.17) | copy-start | bytes 12582916
  96.9 2.2 copy-start.12
  99.1 1.1 copy-start.15
  150.6 4.5 %copy-start.14 = (s32[32]{0:T(128)S(1)}, s32[32]{0:T(128)}, u32[]{:S(2)}) copy-start(s32[32]{0:T(128)} %param.20) | copy-start | bytes 388
  155.2 12.8 %copy-start.8 = (s32[32]{0:T(128)S(1)}, s32[32]{0:T(128)}, u32[]{:S(2)}) copy-start(s32[32]{0:T(128)} %param.21) | copy-start | bytes 388
  166.5 1.4 copy-start
  177.0 4.8 %copy-start.5 = (s32[256,1]{0,1:T(1,128)S(1)}, s32[256,1]{0,1:T(1,128)}, u32[]{:S(2)}) copy-start(s32[256,1]{0,1:T(1,128)} %param.23) | copy-start | bytes 3076
  177.0 43.8 %all-to-all-start.2 = ((bf16[32,3,6,2048]{3,2,1,0:T(8,128)(2,1)}), bf16[32,3,6,2048]{3,2,1,0:T(8,128)(2,1)S(1)}, u32[]{:S(2)}, u32[]{:S(2)}) async-start(bf16[32,3,6,2048]{3,2,1,0:T(8,128)(2,1)} %copy.38), calls=%async_computation.2 | async-start | bytes 6291456 | tf_op jit(solution)/shard_map/all_to_all | solution.py:104
  181.1 23.5 %all-gather.2.cloned.1.call-start = ((), (), s32[]{:S(2)}) async-start(), calls=%async_computation.4 | async-start | bytes 1310720 | tf_op jit(solution)/shard_map/all_gather | solution.py:117
  220.8 33.7 %all-to-all-start = ((bf16[32,16,2048]{2,1,0:T(8,128)(2,1)}), bf16[32,16,2048]{2,1,0:T(8,128)(2,1)}, u32[]{:S(2)}, u32[]{:S(2)}) async-start(bf16[32,16,2048]{2,1,0:T(8,128)(2,1)} %bitcast.132), calls=%async_computation | async-start | bytes 4194304 | tf_op jit(solution)/shard_map/all_to_all | solution.py:122
  227.9 2.9 copy-start.2
  262.1 82.8 %copy-start.1 = (f32[16,3,1,12288]{3,0,1,2:T(8,128)S(1)}, f32[16,3,1,12288]{3,0,1,2:T(8,128)}, u32[]{:S(2)}) copy-start(f32[16,3,1,12288]{3,0,1,2:T(8,128)} %copy-done) | copy-start | bytes 7077892
  339.4 17.2 %all-to-all-start.3 = ((bf16[32,16,512]{2,1,0:T(8,128)(2,1)}), bf16[32,16,512]{2,1,0:T(8,128)(2,1)S(1)}, u32[]{:S(2)}, u32[]{:S(2)}) async-start(bf16[32,16,512]{2,1,0:T(8,128)(2,1)} %bitcast.26), calls=%async_computation.3 | async-start | bytes 1048576 | tf_op jit(solution)/shard_map/all_to_all | solution.py:129
  345.0 3.8 %copy-start.4 = (f32[16,3,1,12288]{3,0,1,2:T(8,128)S(1)}, f32[16,3,1,12288]{3,0,1,2:T(8,128)}, u32[]{:S(2)}) copy-start(f32[16,3,1,12288]{3,0,1,2:T(8,128)} %get-tuple-element.17) | copy-start | bytes 7077892
  348.8 3.8 %copy-start.3 = (f32[16,3,1,12288]{3,0,1,2:T(8,128)S(1)}, f32[16,3,1,12288]{3,0,1,2:T(8,128)}, u32[]{:S(2)}) copy-start(f32[16,3,1,12288]{3,0,1,2:T(8,128)} %get-tuple-element.18) | copy-start | bytes 7077892
Sparse Core Ops, SparseCore 0:
  183.5 21.0 all-gather.1
where the time goes:
time: 365 us
  blocking collectives  197 us (54%)
  waiting for transfers between devices  59.2 us (16%)
  matrix products  40.8 us (11%)
  local copies, waits for them, and re-layouts  36.4 us (10%)
  starting transfers between devices  14.9 us (4%)
  between operations  14.9 us (4%)
    psum x1, blocking collectives, shards(): totals = lax.psum(fwd_partial, 'hid')  75.4 us
    psum x1, blocking collectives, shards(): center = lax.psum(jnp.sum(scores), 'slot') / row_total  66.9 us
    all_to_all x1, blocking collectives, shards(): lax.all_to_all(grads[None].astype(jnp.bfloat16), 'slot', split_axis=2, co...  45.2 us
    all_to_all x1, waiting for transfers between devices, shards(): lax.all_to_all(buffer_rows, 'slot', split_axis=0, concat_axis=0, tiled=True)  23.5 us
    all_gather x1, waiting for transfers between devices, shards(): widened = lax.all_gather(fwd_rows, 'hid', axis=1, tiled=True)  21.8 us
    unnamed x35, local copies, waits for them, and re-layouts  14.4 us
    all_to_all x1, waiting for transfers between devices, shards(): lax.all_to_all(picked, 'slot', split_axis=0, concat_axis=2, tiled=True)[0]  13 us
    dot_general x1, matrix products, shards(): jnp.einsum('es,sabc->eabc', owner_map, arrived, precision=lax.Precision.H...  11.4 us
  transfers between devices with their start and end apart: 4, of which 4 were waited for; matrix products, arithmetic and copies ran while one was open for 6% of the time, Pallas kernels for 0%

commit v1 on v0

--- a/solution.py
+++ b/solution.py
@@ -123,7 +123,10 @@
         buffer_rows, "slot", split_axis=0, concat_axis=0, tiled=True
     ).reshape(slot_count * capacity, widened.shape[1])
     fwd_partial = expert_pass(arrived_rows, resident)[3]
-    totals = lax.psum(fwd_partial, "hid")
+    devices, totals = (lax.axis_size("hid"), fwd_partial)
+    for hop in [1 << k for k in range(devices.bit_length() - 1)]:
+        pairs = [(i, i ^ hop) for i in range(devices)]
+        totals = totals + lax.ppermute(totals, "hid", pairs)
     shares = lax.dynamic_slice_in_dim(totals, lax.axis_index("hid") * quarter, quarter, 1)
     outgoing = shares.astype(jnp.bfloat16).reshape(slot_count, capacity, quarter)
     returned = lax.all_to_all(outgoing, "slot", split_axis=0, concat_axis=0, tiled=True).reshape(

time: 365 us -> 488 us (1.34); the launches traced: 365 us -> 480 us
  waiting for transfers between devices: 59.2 us -> 243 us
  blocking collectives: 197 us -> 122 us
  other arithmetic: 1.62 us -> 9.72 us
    ppermute x0 -> x2, waiting for transfers between devices: none -> 183 us  [shards(): totals = totals + lax.ppermute(totals, 'hid', pairs)]
    psum x1 -> x0, blocking collectives: 75.4 us -> none  [shards(): totals = lax.psum(fwd_partial, 'hid')]
    add x0 -> x1, other arithmetic: none -> 4.92 us  [shards(): totals = totals + lax.ppermute(totals, 'hid', pairs)]
    unnamed x35 -> x33, local copies, waits for them, and re-layouts: 14.4 us -> 13.9 us
  transfers between devices with their start and end apart: 4 -> 6, of which waited for: 4 -> 6; matrix products, arithmetic and copies ran while one was open for 6% -> 4% of each run, Pallas kernels for 0% -> 0%
where the time goes in v1:
time: 488 us; the launch traced here: 480 us
  waiting for transfers between devices  243 us (50%)
  blocking collectives  122 us (25%)
  matrix products  40.8 us (8%)
  local copies, waits for them, and re-layouts  34.1 us (7%)
  starting transfers between devices  16 us (3%)
  between operations  15.3 us (3%)
  other arithmetic  9.72 us (2%)
    ppermute x2, waiting for transfers between devices, shards(): totals = totals + lax.ppermute(totals, 'hid', pairs)  183 us
    psum x1, blocking collectives, shards(): center = lax.psum(jnp.sum(scores), 'slot') / row_total  66.9 us
    all_to_all x1, blocking collectives, shards(): lax.all_to_all(grads[None].astype(jnp.bfloat16), 'slot', split_axis=2, co...  45.4 us
    all_to_all x1, waiting for transfers between devices, shards(): lax.all_to_all(buffer_rows, 'slot', split_axis=0, concat_axis=0, tiled=True)  23.6 us
    all_gather x1, waiting for transfers between devices, shards(): widened = lax.all_gather(fwd_rows, 'hid', axis=1, tiled=True)  21.9 us
    unnamed x33, local copies, waits for them, and re-layouts  13.9 us
    all_to_all x1, waiting for transfers between devices, shards(): lax.all_to_all(picked, 'slot', split_axis=0, concat_axis=2, tiled=True)[0]  13 us
    dot_general x1, matrix products, shards(): jnp.einsum('es,sabc->eabc', owner_map, arrived, precision=lax.Precision.H...  11.4 us
  transfers between devices with their start and end apart: 6, of which 6 were waited for; matrix products, arithmetic and copies ran while one was open for 4% of the time, Pallas kernels for 0%

profile of v1, /device:TPU:1, one launch (start us, length us, event | category | flops | bytes accessed | tf_op | source)
XLA Modules:
  0.0 479.9 jit_solution(17588185481754723676)
XLA Ops:
  7.2 0.7 compare_select_fusion
  7.9 4.1 fusion.16
  11.9 0.0 copy-done.10
  12.0 0.3 copy-done.12
  12.3 2.5 multiply_convert_fusion.2
  14.8 0.0 copy-done.8
  14.8 1.4 fusion.2
  16.2 9.3 %psum.14 = f32[1024]{0:T(1024)S(1)} all-reduce(f32[1024]{0:T(1024)S(1)} %fusion.2), channel_id=1, replica_groups=mesh['slot'=32,'hid'=4] {'hid'}, use_global_device_ids=true, to_apply=%region_4.5 | all-reduce | flops 1024 | bytes 8192 | tf_op jit(solution)/shard_map/psum | solution.py:81
  25.5 0.0 copy-done.6
  25.5 0.6 fusion.79
  26.1 66.9 %psum.15 = f32[]{:T(128)} all-reduce(f32[]{:T(128)} %get-tuple-element.19), channel_id=1, replica_groups=mesh['slot'=32,'hid'=4] {'slot'}, use_global_device_ids=true, to_apply=%region_6.7 | all-reduce | flops 1 | bytes 8 | tf_op jit(solution)/shard_map/psum | solution.py:84
  93.6 0.0 copy-start.9
  93.6 3.4 fusion.35
  97.1 0.0 copy-done.9
  97.1 1.6 fusion.6
  98.7 0.5 copy-done.11
  99.3 1.1 fusion.29
  100.4 0.1 copy-done.14
  100.4 1.2 fusion.32
  101.6 0.3 pad_maximum_fusion
  101.9 2.0 copy.33
  103.9 45.4 %all_to_all.40 = bf16[1,3,192,2048]{3,1,0,2:T(4,128)(2,1)S(1)} all-to-all(bf16[1,3,192,2048]{3,1,0,2:T(4,128)(2,1)S(1)} %copy.33), channel_id=1, replica_groups=mesh['slot'=32,'hid'=4] {'slot'}, dimensions={2} | all-to-all | bytes 4718592 | tf_op jit(solution)/shard_map/all_to_all | solution.py:87
  149.3 1.7 copy.55
  151.0 0.0 copy-start.13
  151.0 4.5 reshape.144
  155.5 0.0 copy-done.13
  155.5 11.4 %multiply_subtract_fusion = (f32[16,3,1,12288]{3,0,1,2:T(8,128)S(1)}, f32[16,3,1,12288]{3,0,1,2:T(8,128)}, f32[16,3,1,12288]{3,0,1,2:T(8,128)}) fusion(f32[16,3,1,12288]{3,2,1,0:T(1,128)} %param.12, f32[16,3,1,12288]{3,2,1,0:T(1,128)} %param.13, f32[16,3,1,12288]{3,2,1,0:T(1,128)} %param.14, bf16[32,3,12288]{2,0,1:T(8,128)(2,1)} %reshape.144, ...), kind=kOutput, calls=%fused_computation.36 | convolution fusion | flops 46596608 | bytes 16515200 | tf_op jit(solution)/shard_map/es,sabc->eabc/dot_general | solution.py:94
  166.9 1.4 copy-done
  168.3 0.0 copy-done.7
  168.3 2.2 convolution_convert_fusion
  170.5 5.0 %reshape.146 = bf16[32,3,6,2048]{3,2,0,1:T(8,128)(2,1)S(1)} reshape(bf16[32,3,12288]{2,0,1:T(8,128)(2,1)} %convolution_convert_fusion) | data formatting | bytes 4718592 | tf_op jit(solution)/shard_map/reshape | solution.py:103
  175.5 1.9 copy.38
  177.4 4.0 all-to-all-start.2
  181.4 0.0 all-gather.2.cloned.1.call-start
  181.5 0.7 all-gather.2.cloned.1.call-update
  182.2 0.0 copy-done.5
  182.2 0.6 reduce-window.6
  182.8 0.2 slice_reduce_fusion
  183.0 0.1 fusion.65
  183.1 21.9 %all-gather.2.cloned.1.call-done = bf16[256,2048]{1,0:T(8,128)(2,1)} async-done(((bf16[256,512]{1,0:T(8,128)(2,1)}), bf16[256,2048]{1,0:T(8,128)(2,1)}) %all-gather.2.cloned.1.call-update) | async-done | bytes 1048592 | tf_op jit(solution)/shard_map/all_gather | solution.py:117
  205.0 3.3 convolution_convert_fusion.1
  208.3 13.0 %all-to-all-done.2 = bf16[32,3,6,2048]{3,2,1,0:T(8,128)(2,1)S(1)} async-done(((bf16[32,3,6,2048]{3,2,1,0:T(8,128)(2,1)}), bf16[32,3,6,2048]{3,2,1,0:T(8,128)(2,1)S(1)}, u32[]{:S(2)}, u32[]{:S(2)}) %all-to-all-start.2) | async-done | bytes 2359328 | tf_op jit(solution)/shard_map/all_to_all | solution.py:104
  221.2 5.3 %all-to-all-start = ((bf16[32,16,2048]{2,1,0:T(8,128)(2,1)}), bf16[32,16,2048]{2,1,0:T(8,128)(2,1)}, u32[]{:S(2)}, u32[]{:S(2)}) async-start(bf16[32,16,2048]{2,1,0:T(8,128)(2,1)} %bitcast.132), calls=%async_computation | async-start | bytes 4194304 | tf_op jit(solution)/shard_map/all_to_all | solution.py:122
  226.5 1.7 fusion.80
  228.2 1.5 squeeze.38
  229.7 1.4 squeeze.40
  231.2 0.3 squeeze.39
  231.4 23.6 %all-to-all-done = bf16[32,16,2048]{2,1,0:T(8,128)(2,1)} async-done(((bf16[32,16,2048]{2,1,0:T(8,128)(2,1)}), bf16[32,16,2048]{2,1,0:T(8,128)(2,1)}, u32[]{:S(2)}, u32[]{:S(2)}) %all-to-all-start) | async-done | bytes 2097184 | tf_op jit(solution)/shard_map/all_to_all | solution.py:122
  255.0 2.4 fusion.81
  257.4 5.1 %fusion.43 = f32[512,2048]{1,0:T(8,128)} fusion(bf16[192,2048]{1,0:T(8,128)(2,1)S(1)} %squeeze.40, bf16[512,2048]{1,0:T(8,128)(2,1)} %bitcast.4, bf16[192,2048]{1,0:T(8,128)(2,1)S(1)} %squeeze.39, f32[512,192]{0,1:T(8,128)S(1)} %fusion.81), kind=kOutput, calls=%fused_computation.42 | convolution fusion | flops 805896192 | bytes 8257536 | tf_op jit(solution)/shard_map/dot_general | solution.py:23
  262.6 0.0 collective-permute-start
  262.6 91.5 %collective-permute-done = f32[512,2048]{1,0:T(8,128)S(1)} collective-permute-done((f32[512,2048]{1,0:T(8,128)}, f32[512,2048]{1,0:T(8,128)S(1)}, u32[]{:S(2)}, u32[]{:S(2)}) %collective-permute-start) | collective-permute-done | bytes 4194336 | tf_op jit(solution)/shard_map/ppermute | solution.py:129
  354.1 4.9 %add.58 = f32[512,2048]{1,0:T(8,128)} add(f32[512,2048]{1,0:T(8,128)} %fusion.43, f32[512,2048]{1,0:T(8,128)S(1)} %collective-permute-done) | non-fusion elementwise | flops 1048576 | bytes 12582912 | tf_op jit(solution)/shard_map/add | solution.py:129
  359.0 0.6 collective-permute-start.1
  359.6 91.7 %collective-permute-done.1 = f32[512,2048]{1,0:T(8,128)} collective-permute-done((f32[512,2048]{1,0:T(8,128)}, f32[512,2048]{1,0:T(8,128)}, u32[]{:S(2)}, u32[]{:S(2)}) %collective-permute-start.1) | collective-permute-done | bytes 4194336 | tf_op jit(solution)/shard_map/ppermute | solution.py:129
  451.3 2.5 fusion.44
  453.8 6.1 %all-to-all-start.3 = ((bf16[32,16,512]{2,1,0:T(8,128)(2,1)}), bf16[32,16,512]{2,1,0:T(8,128)(2,1)S(1)}, u32[]{:S(2)}, u32[]{:S(2)}) async-start(bf16[32,16,512]{2,1,0:T(8,128)(2,1)} %bitcast.26), calls=%async_computation.3 | async-start | bytes 1048576 | tf_op jit(solution)/shard_map/all_to_all | solution.py:132
  459.9 0.0 copy-start.4
  459.9 3.8 copy.39
  463.7 3.8 copy.40
  467.6 0.0 copy-done.3
  467.6 3.8 copy.41
  471.4 0.2 all-to-all-done.3
  471.6 1.1 convolution_convert_fusion.2
  (20 shorter events, 0.1 us)
Async XLA Ops:
  7.9 4.1 copy-start.10
  7.9 4.4 copy-start.12
  12.3 2.5 copy-start.8
  14.8 10.7 %copy-start.6 = (f32[1,1024]{1,0:T(1,128)S(1)}, f32[1,1024]{1,0:T(1,128)}, u32[]{:S(2)}) copy-start(f32[1,1024]{1,0:T(1,128)} %param.18) | copy-start | bytes 12292
  93.6 3.5 copy-start.9
  97.1 2.2 copy-start.11
  99.3 1.1 copy-start.14
  151.0 4.5 copy-start.13
  155.5 12.8 %copy-start.7 = (s32[32]{0:T(128)S(1)}, s32[32]{0:T(128)}, u32[]{:S(2)}) copy-start(s32[32]{0:T(128)} %param.21) | copy-start | bytes 388
  166.9 1.4 copy-start
  177.4 4.8 copy-start.5
  177.4 43.8 %all-to-all-start.2 = ((bf16[32,3,6,2048]{3,2,1,0:T(8,128)(2,1)}), bf16[32,3,6,2048]{3,2,1,0:T(8,128)(2,1)S(1)}, u32[]{:S(2)}, u32[]{:S(2)}) async-start(bf16[32,3,6,2048]{3,2,1,0:T(8,128)(2,1)} %copy.38), calls=%async_computation.2 | async-start | bytes 6291456 | tf_op jit(solution)/shard_map/all_to_all | solution.py:104
  181.4 23.6 %all-gather.2.cloned.1.call-start = ((), (), s32[]{:S(2)}) async-start(), calls=%async_computation.4 | async-start | bytes 1310720 | tf_op jit(solution)/shard_map/all_gather | solution.py:117
  221.2 33.7 %all-to-all-start = ((bf16[32,16,2048]{2,1,0:T(8,128)(2,1)}), bf16[32,16,2048]{2,1,0:T(8,128)(2,1)}, u32[]{:S(2)}, u32[]{:S(2)}) async-start(bf16[32,16,2048]{2,1,0:T(8,128)(2,1)} %bitcast.132), calls=%async_computation | async-start | bytes 4194304 | tf_op jit(solution)/shard_map/all_to_all | solution.py:122
  228.2 2.9 copy-start.2
  262.6 91.5 %collective-permute-start = (f32[512,2048]{1,0:T(8,128)}, f32[512,2048]{1,0:T(8,128)S(1)}, u32[]{:S(2)}, u32[]{:S(2)}) collective-permute-start(f32[512,2048]{1,0:T(8,128)} %fusion.43), channel_id=1, source_target_pairs={{0,1},{1,0},{2,3},{3,2},{4,5},{5,4},{6,7},{7,6},{8,9},{9,8},{10,11... | collective-permute-start | bytes 12582920 | tf_op jit(solution)/shard_map/ppermute | solution.py:129
  359.0 100.9 %copy-start.1 = (f32[16,3,1,12288]{3,0,1,2:T(8,128)S(1)}, f32[16,3,1,12288]{3,0,1,2:T(8,128)}, u32[]{:S(2)}) copy-start(f32[16,3,1,12288]{3,0,1,2:T(8,128)} %copy-done) | copy-start | bytes 7077892
  359.0 92.3 %collective-permute-start.1 = (f32[512,2048]{1,0:T(8,128)}, f32[512,2048]{1,0:T(8,128)}, u32[]{:S(2)}, u32[]{:S(2)}) collective-permute-start(f32[512,2048]{1,0:T(8,128)} %add.58), channel_id=1, source_target_pairs={{0,2},{1,3},{2,0},{3,1},{4,6},{5,7},{6,4},{7,5},{8,10},{9,11},{10,... | collective-permute-start | bytes 12582920 | tf_op jit(solution)/shard_map/ppermute | solution.py:129
  453.8 17.8 %all-to-all-start.3 = ((bf16[32,16,512]{2,1,0:T(8,128)(2,1)}), bf16[32,16,512]{2,1,0:T(8,128)(2,1)S(1)}, u32[]{:S(2)}, u32[]{:S(2)}) async-start(bf16[32,16,512]{2,1,0:T(8,128)(2,1)} %bitcast.26), calls=%async_computation.3 | async-start | bytes 1048576 | tf_op jit(solution)/shard_map/all_to_all | solution.py:132
  459.9 3.8 copy-start.4
  463.7 3.8 copy-start.3
Sparse Core Ops, SparseCore 0:
  183.9 21.0 all-gather.1
